TPU v7x, 512 devices: a whole 4x4x16 slice. The times are simulated.
512 devices in a mesh: ctx: 64 (over x, z), head: 8 (over y, core).
Axes of the slice: x: 4, y: 4, z: 16, core: 2. Of those that a mesh axis runs over, the one named last changes fastest.
Arguments:
- hidden_in: bfloat16 [65536, 2048], P('ctx', 'head'), may hold values from -6 to 6
- proj_weight: bfloat16 [2048, 3584], P(None, 'head'), may hold values from -0.125 to 0.125
- conv_weight: float32 [3, 1024], P(None, 'head'), may hold values from -3 to 3
- norm_gain: float32 [1024], P('head'), may hold values from 0.1 to 1.9
- out_weight: bfloat16 [1024, 2048], P('head'), may hold values from -0.25 to 0.25
Outputs:
- layer_out: bfloat16 [65536, 2048], P('ctx', 'head')
All inputs are finite; a program needn't handle non-finite values.
Results may differ from a plain program's by a relative error of at most 0.014.
Values may be sent and summed in bfloat16 or wider, within the bound.
A program may use at most 64 MiB of HBM per device.

v0:
```python
import jax
import jax.numpy as jnp
from jax import lax
from jax.sharding import PartitionSpec as P

DV = 64
FQK = 16
WIN = 64
CONV = 3


def shifted(value, axis, by):
    count = lax.axis_size(axis)
    pairs = [(i, i + by) for i in range(count) if 0 <= i + by < count]
    return lax.ppermute(value, axis, pairs)


def features(vector):
    vec_len = vector.shape[-1]
    square = (vector[..., :, None] * vector[..., None, :]).reshape(
        vector.shape[:-1] + (vec_len * vec_len,)
    )
    constant = jnp.ones(vector.shape[:-1] + (1,), vector.dtype)
    return jnp.concatenate(
        [constant, vector / vec_len**0.25, square / (2.0 * vec_len) ** 0.5], axis=-1
    )


def normalize(block_in):
    values = block_in.astype(jnp.float32)
    return (values * lax.rsqrt(jnp.mean(values * values, axis=-1, keepdims=True) + 1e-06)).astype(
        jnp.bfloat16
    )


def convolve(extended, conv_weight, count):
    tap_count = conv_weight.shape[0]
    total = jnp.zeros((count, extended.shape[1]), jnp.float32)
    for tap_id in range(tap_count):
        offset = tap_count - 1 - tap_id
        total = total + conv_weight[tap_id] * extended[offset : offset + count].astype(jnp.float32)
    return total.astype(jnp.bfloat16)


def per_device(hidden_in, proj_weight, conv_weight, norm_gain, out_weight):
    highest = lax.Precision.HIGHEST
    row_count = hidden_in.shape[0]
    head_count = out_weight.shape[0] // DV
    per_head = 2 * FQK + 3 * DV
    reach_rows = WIN - 1
    edge_rows = CONV - 1
    projected = jnp.dot(
        lax.all_gather(hidden_in, "head", axis=1, tiled=True),
        proj_weight,
        preferred_element_type=jnp.float32,
    ).astype(jnp.bfloat16)
    projected = projected.reshape(row_count, head_count, per_head)
    lin_query = projected[:, :, :FQK]
    lin_key = projected[:, :, FQK : 2 * FQK]
    raw_values = projected[:, :, 2 * FQK : 2 * FQK + DV].reshape(row_count, head_count * DV)
    win_query = projected[:, :, 2 * FQK + DV : 2 * FQK + 2 * DV]
    win_key = projected[:, :, 2 * FQK + 2 * DV :].reshape(row_count, head_count * DV)
    before_rows = shifted(raw_values[row_count - edge_rows :], "ctx", 1)
    conv_values = convolve(jnp.concatenate([before_rows, raw_values], 0), conv_weight, row_count)
    prev_values, prev_keys = shifted(
        (conv_values[row_count - reach_rows :], win_key[row_count - reach_rows :]), "ctx", 1
    )
    value_grid = conv_values.reshape(row_count, head_count, DV)
    value_full = value_grid.astype(jnp.float32)
    key_feat = features(lin_key.astype(jnp.float32))
    own_state = jnp.einsum("thf,thd->fhd", key_feat, value_full, precision=highest)
    feat_count = own_state.shape[0]
    flat_state = own_state.reshape(feat_count, head_count * DV)
    position = lax.axis_index("ctx")
    piece = lax.all_gather(flat_state[None], "ctx", axis=0, tiled=True)
    shard_ids = jnp.arange(piece.shape[0], dtype=jnp.int32)
    lower_mask = (shard_ids < position)[:, None, None]
    prior = jnp.sum(jnp.where(lower_mask, piece, 0.0), axis=0)
    prior_grid = prior.reshape(feat_count, head_count, DV)
    query_feat = features(lin_query.astype(jnp.float32))
    carried = jnp.einsum("thf,fhd->thd", query_feat, prior_grid, precision=highest)
    block_rows = min(row_count, 512)
    block_total = row_count // block_rows
    key_pos = jnp.arange(row_count, dtype=jnp.int32)

    def local_block(block_id):
        offset = block_id * block_rows
        query_part = lax.dynamic_slice_in_dim(lin_query, offset, block_rows, 0)
        products = jnp.einsum(
            "thf,shf->hts", query_part, lin_key, preferred_element_type=jnp.float32
        )
        scaled = products / FQK**0.5
        query_pos = offset + jnp.arange(block_rows, dtype=jnp.int32)
        visible = key_pos[None, :] <= query_pos[:, None]
        kernel = jnp.where(visible[None], 1.0 + scaled + 0.5 * scaled * scaled, 0.0).astype(
            jnp.bfloat16
        )
        return jnp.einsum("hts,shd->thd", kernel, value_grid, preferred_element_type=jnp.float32)

    own_part = lax.map(local_block, jnp.arange(block_total, dtype=jnp.int32)).reshape(
        row_count, head_count, DV
    )
    lin = carried + own_part
    ext_keys = normalize(
        jnp.concatenate([prev_keys, win_key], 0).reshape(row_count + reach_rows, head_count, DV)
    )
    ext_values = jnp.concatenate([prev_values, conv_values], 0).reshape(
        row_count + reach_rows, head_count, DV
    )
    query_norm = normalize(win_query)
    first_token = position * row_count
    shift_ids = (
        jnp.arange(block_rows + reach_rows, dtype=jnp.int32)[None, :]
        - jnp.arange(block_rows, dtype=jnp.int32)[:, None]
    )
    band = (shift_ids >= 0) & (shift_ids <= reach_rows)

    def window_block(block_id):
        offset = block_id * block_rows
        query_part = lax.dynamic_slice_in_dim(query_norm, offset, block_rows, 0)
        key_part = lax.dynamic_slice_in_dim(ext_keys, offset, block_rows + reach_rows, 0)
        value_part = lax.dynamic_slice_in_dim(ext_values, offset, block_rows + reach_rows, 0)
        scores = (
            jnp.einsum("thd,shd->hts", query_part, key_part, preferred_element_type=jnp.float32)
            / DV**0.5
        )
        global_pos = (
            first_token + offset + jnp.arange(block_rows + reach_rows, dtype=jnp.int32) - reach_rows
        )
        allowed = band & (global_pos >= 0)[None, :]
        expo = jnp.where(allowed[None], jnp.exp(scores), 0.0)
        weights = (expo / jnp.sum(expo, axis=-1, keepdims=True)).astype(jnp.bfloat16)
        return jnp.einsum("hts,shd->thd", weights, value_part, preferred_element_type=jnp.float32)

    window = lax.map(window_block, jnp.arange(block_total, dtype=jnp.int32)).reshape(
        row_count, head_count, DV
    )
    mean_sq = jnp.mean(lin * lin, axis=-1, keepdims=True)
    gain_grid = norm_gain.reshape(head_count, DV)
    mixed_heads = (lin * lax.rsqrt(mean_sq + 1e-05) * gain_grid + window).astype(jnp.bfloat16)
    mixed_flat = mixed_heads.reshape(row_count, head_count * DV)
    partial_out = jnp.dot(mixed_flat, out_weight, preferred_element_type=jnp.float32)
    return lax.psum_scatter(
        partial_out.astype(jnp.bfloat16), "head", scatter_dimension=1, tiled=True
    )


def solution(mesh):
    return jax.shard_map(
        per_device,
        mesh=mesh,
        in_specs=(P("ctx", "head"), P(None, "head"), P(None, "head"), P("head"), P("head", None)),
        out_specs=P("ctx", "head"),
        check_vma=False,
    )
```

profile of v0, /device:TPU:4, one launch (start us, length us, event | category | flops | bytes accessed | tf_op | source)
XLA Modules:
  0.0 292.0 jit_solution(8523061620894326594)
XLA Ops:
  6.5 0.7 all-gather.3.cloned.1.call-update
  7.3 0.0 all-gather.5.cloned.1.call-start
  7.3 0.8 slice_bitcast_fusion.2
  8.1 49.0 %all-gather.3.cloned.1.call-done = bf16[1024,2048]{1,0:T(8,128)(2,1)} async-done(((bf16[1024,256]{1,0:T(8,128)(2,1)}), bf16[1024,2048]{1,0:T(8,128)(2,1)}) %all-gather.3.cloned.1.call-update) | async-done | bytes 4194320 | tf_op jit(solution)/shard_map/all_gather | solution.py:53
  57.1 4.3 %convolution_convert_fusion.1 = bf16[1024,448]{0,1:T(8,128)(2,1)S(1)} fusion(bf16[1024,2048]{1,0:T(8,128)(2,1)} %all-gather.3.cloned.1.call-done, bf16[2048,448]{0,1:T(8,128)(2,1)S(1)} %copy-done), kind=kOutput, calls=%fused_computation.46 | convolution fusion | flops 1879506944 | bytes 6946816 | tf_op jit(solution)/shard_map/dot_general | solution.py:52
  61.4 0.1 slice.63
  61.5 0.7 slice_convert_fusion
  62.2 3.5 %collective-permute-start = (bf16[2,128]{0,1:T(8,128)(2,1)S(1)}, bf16[2,128]{0,1:T(8,128)(2,1)S(1)}, u32[]{:S(2)}, u32[]{:S(2)}) collective-permute-start(bf16[2,128]{0,1:T(8,128)(2,1)S(1)} %bitcast.73), channel_id=1, source_target_pairs={{0,8},{8,16},{16,24},{24,32},{32,40},{40,48},{48,56},{56,64},{64,7... | collective-permute-start | bytes 1544 | tf_op jit(solution)/shard_map/ppermute | solution.py:15
  65.7 0.3 multiply_multiply_fusion.1
  66.0 4.1 %collective-permute-done = bf16[2,128]{0,1:T(8,128)(2,1)S(1)} collective-permute-done((bf16[2,128]{0,1:T(8,128)(2,1)S(1)}, bf16[2,128]{0,1:T(8,128)(2,1)S(1)}, u32[]{:S(2)}, u32[]{:S(2)}) %collective-permute-start) | collective-permute-done | bytes 544 | tf_op jit(solution)/shard_map/ppermute | solution.py:15
  70.1 1.1 add_convert_fusion.1
  71.2 2.5 fusion.29
  73.7 0.8 copy.15
  74.5 0.0 all-gather.5.cloned.1.call-update
  74.5 0.0 reduce-scatter.2.cloned.1.call-start
  74.6 0.1 mul.156
  74.7 0.7 slice.70
  75.3 1.9 collective-permute-start.2
  77.3 0.1 fusion.49
  77.4 0.8 fusion.50
  78.1 1.6 multiply_multiply_fusion
  79.7 1.4 slice.68
  81.2 3.1 %collective-permute-start.1 = (bf16[63,128]{0,1:T(8,128)(2,1)}, bf16[63,128]{0,1:T(8,128)(2,1)}, u32[]{:S(2)}, u32[]{:S(2)}) collective-permute-start(bf16[63,128]{0,1:T(8,128)(2,1)} %slice.68), channel_id=1, source_target_pairs={{0,8},{8,16},{16,24},{24,32},{32,40},{40,48},{48,56},{56,64},{64,7... | collective-permute-start | bytes 48392 | tf_op jit(solution)/shard_map/ppermute | solution.py:15
  84.2 0.1 broadcast.170.clone2.1
  84.4 14.3 %while.26 = (s32[]{:T(128)}, f32[2,512,2,64]{1,0,3,2:T(2,128)S(1)}, s32[2]{0:T(128)S(1)}, bf16[1024,2,16]{0,2,1:T(8,128)(2,1)}, bf16[1024,2,16]{0,2,1:T(8,128)(2...) while((s32[]{:T(128)}, f32[2,512,2,64]{1,0,3,2:T(2,128)S(1)}, ...), condition=%wide.region_2.3_spmd.clone, body=%wide.region_1.2_spmd.clone.sunk | while | flops 175636992 | bytes 2724019 | solution.py:100
  84.4 0.6 dynamic_slice.63
  85.7 0.4 iota_compare_fusion.3
  86.0 2.7 fusion.74
  88.8 0.3 copy.29
  89.1 2.4 dynamic_update_slice.17
  91.5 0.6 dynamic_slice.63
  92.8 0.4 iota_compare_fusion.3
  93.2 2.7 fusion.74
  95.9 0.3 copy.29
  96.2 2.4 dynamic_update_slice.17
  98.7 1.2 reshape.143
  99.9 0.9 fusion.47
  100.9 0.9 fusion.48
  101.8 1.1 pad_maximum_fusion
  102.9 0.1 broadcast.170.clone2
  103.0 14.0 %while.27 = (s32[]{:T(128)}, f32[2,512,2,64]{1,0,3,2:T(2,128)S(1)}, s32[2]{0:T(128)S(1)}, bf16[1087,2,64]{0,2,1:T(8,128)(2,1)S(1)}, s32[]{:T(128)}, /*index=5*/b...) while((s32[]{:T(128)}, f32[2,512,2,64]{1,0,3,2:T(2,128)S(1)}, ...), condition=%wide.region_8.9_spmd.clone, body=%wide.region_6.8_spmd.clone.sunk | while | flops 156327104 | bytes 7377774 | solution.py:135
  103.0 0.7 dynamic_slice.67
  104.4 0.2 fusion.76
  104.6 1.9 fusion.77
  106.5 0.8 fusion.78
  107.3 0.3 copy.30
  107.6 2.4 dynamic_update_slice.18
  110.1 0.7 dynamic_slice.67
  111.4 0.2 fusion.76
  111.6 1.9 fusion.77
  113.5 0.8 fusion.78
  114.3 0.3 copy.30
  114.6 2.4 dynamic_update_slice.18
  117.1 0.5 reshape.145
  117.5 0.0 copy-start.1
  117.5 114.2 %all-gather.5.cloned.1.call-done = f32[64,273,128]{2,1,0:T(8,128)} async-done(((f32[1,273,128]{2,1,0:T(8,128)}), f32[64,273,128]{2,1,0:T(8,128)}) %all-gather.5.cloned.1.call-update) | async-done | bytes 8945680 | tf_op jit(solution)/shard_map/all_gather | solution.py:75
  231.8 4.7 %select_reduce_fusion = f32[273,128]{1,0:T(8,128)S(1)} fusion(f32[64,273,128]{2,1,0:T(8,128)} %all-gather.5.cloned.1.call-done, pred[64]{0:T(512)(128)(4,1)S(1)} %iota_compare_fusion.1), kind=kLoop, calls=%fused_computation.32 | loop fusion | flops 4437888 | bytes 9085504 | tf_op jit(solution)/shard_map/reduce_sum | solution.py:78
  236.4 0.1 copy.16
  236.6 0.0 copy-start.2
  236.6 3.7 %multiply_reduce_fusion = (f32[1024,2]{0,1:T(2,128)S(1)}, f32[1024,2,64]{0,2,1:T(8,128)S(1)}) fusion(f32[1024,2,64]{0,2,1:T(8,128)S(1)} %copy-done.1, f32[273,2,64]{0,2,1:T(8,128)S(1)} %bitcast.70, f32[1024,2,256]{0,2,1:T(8,128)} %bitcast.59, f32[1024,2,16]{0,2,1:T(8,128)S(1)} %get-tuple-element.255, f32[273]{0:T(512)S(1)} %pad.7.clone), kind=kOutput, calls=%fused_computation.60 | convolution fusion | flops 430901248 | bytes 3425860 | tf_op jit(solution)/shard_map/thf,fhd->thd/dot_general | solution.py:81
  240.4 0.1 add_convert_fusion
  240.5 3.2 %convolution_convert_fusion = bf16[1024,2048]{1,0:T(8,128)(2,1)} fusion(bf16[1024,128]{0,1:T(8,128)(2,1)S(1)} %bitcast.68, bf16[128,2048]{1,0:T(8,128)(2,1)S(1)} %copy-done.2), kind=kOutput, calls=%fused_computation.33 | convolution fusion | flops 538968064 | bytes 4980736 | tf_op jit(solution)/shard_map/dot_general | solution.py:142
  243.7 0.0 reduce-scatter.2.cloned.1.call-update
  243.7 41.7 %reduce-scatter.2.cloned.1.call-done = bf16[1024,256]{1,0:T(8,128)(2,1)} async-done(((bf16[1024,2048]{1,0:T(8,128)(2,1)}), bf16[1024,256]{1,0:T(8,128)(2,1)}) %reduce-scatter.2.cloned.1.call-update) | async-done | bytes 524304 | tf_op jit(solution)/shard_map/reduce_scatter | solution.py:143
  (22 shorter events, 0.2 us)
Async XLA Ops:
  6.5 50.6 %copy-start = (bf16[2048,448]{0,1:T(8,128)(2,1)S(1)}, bf16[2048,448]{0,1:T(8,128)(2,1)}, u32[]{:S(2)}) copy-start(bf16[2048,448]{0,1:T(8,128)(2,1)} %param.10) | copy-start | bytes 5505028
  6.5 50.6 %all-gather.3.cloned.1.call-start = ((), (), s32[]{:S(2)}) async-start(), calls=%async_computation.1 | async-start | bytes 4718592 | tf_op jit(solution)/shard_map/all_gather | solution.py:53
  7.3 224.5 %all-gather.5.cloned.1.call-start = ((), (), s32[]{:S(2)}) async-start(), calls=%async_computation.2 | async-start | bytes 9318400 | tf_op jit(solution)/shard_map/all_gather | solution.py:75
  62.2 7.9 %collective-permute-start = (bf16[2,128]{0,1:T(8,128)(2,1)S(1)}, bf16[2,128]{0,1:T(8,128)(2,1)S(1)}, u32[]{:S(2)}, u32[]{:S(2)}) collective-permute-start(bf16[2,128]{0,1:T(8,128)(2,1)S(1)} %bitcast.73), channel_id=1, source_target_pairs={{0,8},{8,16},{16,24},{24,32},{32,40},{40,48},{48,56},{56,64},{64,7... | collective-permute-start | bytes 1544 | tf_op jit(solution)/shard_map/ppermute | solution.py:15
  65.9 8.6 %copy-start.3 = (f32[128]{0:T(128)S(1)}, f32[128]{0:T(128)}, u32[]{:S(2)}) copy-start(f32[128]{0:T(128)} %param.12) | copy-start | bytes 1540
  74.5 211.0 %reduce-scatter.2.cloned.1.call-start = ((), (), s32[]{:S(2)}) async-start(), calls=%async_computation.3 | async-start | bytes 4718592 | tf_op jit(solution)/shard_map/reduce_scatter | solution.py:143
  75.3 24.6 %collective-permute-start.2 = (bf16[63,128]{0,1:T(8,128)(2,1)}, bf16[63,128]{0,1:T(8,128)(2,1)}, u32[]{:S(2)}, u32[]{:S(2)}) collective-permute-start(bf16[63,128]{0,1:T(8,128)(2,1)} %bitcast.14), channel_id=1, source_target_pairs={{0,8},{8,16},{16,24},{24,32},{32,40},{40,48},{48,56},{56,64},{64,7... | collective-permute-start | bytes 48392 | tf_op jit(solution)/shard_map/ppermute | solution.py:15
  81.2 20.6 %collective-permute-start.1 = (bf16[63,128]{0,1:T(8,128)(2,1)}, bf16[63,128]{0,1:T(8,128)(2,1)}, u32[]{:S(2)}, u32[]{:S(2)}) collective-permute-start(bf16[63,128]{0,1:T(8,128)(2,1)} %slice.68), channel_id=1, source_target_pairs={{0,8},{8,16},{16,24},{24,32},{32,40},{40,48},{48,56},{56,64},{64,7... | collective-permute-start | bytes 48392 | tf_op jit(solution)/shard_map/ppermute | solution.py:15
  117.5 119.1 %copy-start.1 = (f32[1024,2,64]{0,2,1:T(8,128)S(1)}, f32[1024,2,64]{0,2,1:T(8,128)}, u32[]{:S(2)}) copy-start(f32[1024,2,64]{0,2,1:T(8,128)} %reshape.143) | copy-start | bytes 1572868
  236.6 3.9 %copy-start.2 = (bf16[128,2048]{1,0:T(8,128)(2,1)S(1)}, bf16[128,2048]{1,0:T(8,128)(2,1)}, u32[]{:S(2)}) copy-start(bf16[128,2048]{1,0:T(8,128)(2,1)} %param.13) | copy-start | bytes 1572868
Sparse Core Ops, SparseCore 0:
  9.4 47.6 all-gather.2
  74.6 157.0 all-gather.4
  243.9 41.5 reduce-scatter.1
where the time goes:
time: 293 us; the launch traced here: 292 us
  waiting for transfers between devices  210 us (72%)
  matrix products  24.6 us (8%)
  local copies, waits for them, and re-layouts  19.4 us (7%)
  other arithmetic  13.4 us (5%)
  between operations  13.3 us (5%)
  starting transfers between devices  8.51 us (3%)
    all_gather x1, waiting for transfers between devices, per_device(): piece = lax.all_gather(flat_state[None], 'ctx', axis=0, tiled=True)  114 us
    all_gather x1, waiting for transfers between devices, per_device(): lax.all_gather(hidden_in, 'head', axis=1, tiled=True)  49 us
    reduce_scatter x1, waiting for transfers between devices, per_device(): lax.psum_scatter(partial_out.astype(jnp.bfloat16), 'head', scatter_dimens...  41.7 us
    dynamic_update_slice x8, local copies, waits for them, and re-layouts, per_device(): lax.map(local_block, jnp.arange(block_total, dtype=jnp.int32))  10.9 us
    ppermute x3, starting transfers between devices, shifted(): return lax.ppermute(value, axis, pairs)  8.42 us
  transfers between devices with their start and end apart: 6, of which 4 were waited for; matrix products, arithmetic and copies ran while one was open for 12% of the time, Pallas kernels for 0%

commit v1 on v0

--- a/solution.py
+++ b/solution.py
@@ -72,7 +72,9 @@
     feat_count = own_state.shape[0]
     flat_state = own_state.reshape(feat_count, head_count * DV)
     position = lax.axis_index("ctx")
-    piece = lax.all_gather(flat_state[None], "ctx", axis=0, tiled=True)
+    piece = jnp.concatenate(
+        lax.all_to_all(jnp.stack([flat_state[None]] * lax.axis_size("ctx")), "ctx", 0, 0), axis=0
+    )
     shard_ids = jnp.arange(piece.shape[0], dtype=jnp.int32)
     lower_mask = (shard_ids < position)[:, None, None]
     prior = jnp.sum(jnp.where(lower_mask, piece, 0.0), axis=0)

time: 293 us -> 564 us (1.92)
  the two profiles are of different devices: /device:TPU:4 before, /device:TPU:2 now
where the time goes in v1:
time: 564 us
  waiting for transfers between devices  457 us (81%)
  local copies, waits for them, and re-layouts  25.5 us (5%)
  starting transfers between devices  25.5 us (5%)
  matrix products  25.3 us (4%)
  other arithmetic  14.1 us (2%)
  between operations  13.7 us (2%)
    ppermute x3, waiting for transfers between devices, shifted(): return lax.ppermute(value, axis, pairs)  361 us
    all_gather x1, waiting for transfers between devices, per_device(): lax.all_gather(hidden_in, 'head', axis=1, tiled=True)  49.1 us
    reduce_scatter x1, waiting for transfers between devices, per_device(): lax.psum_scatter(partial_out.astype(jnp.bfloat16), 'head', scatter_dimens...  46.2 us
    all_to_all x1, starting transfers between devices, per_device(): lax.all_to_all(jnp.stack([flat_state[None]] * lax.axis_size('ctx')), 'ctx...  15.1 us
  transfers between devices with their start and end apart: 6, of which 4 were waited for; matrix products, arithmetic and copies ran while one was open for 6% of the time, Pallas kernels for 0%

profile of v1, /device:TPU:2, one launch (start us, length us, event | category | flops | bytes accessed | tf_op | source)
XLA Modules:
  0.0 563.8 jit_solution(12853094850958260970)
XLA Ops:
  6.5 0.7 all-gather.2.cloned.1.call-update
  7.3 0.8 slice_bitcast_fusion.2
  8.1 49.1 %all-gather.2.cloned.1.call-done = bf16[1024,2048]{1,0:T(8,128)(2,1)} async-done(((bf16[1024,256]{1,0:T(8,128)(2,1)}), bf16[1024,2048]{1,0:T(8,128)(2,1)}) %all-gather.2.cloned.1.call-update) | async-done | bytes 4194320 | tf_op jit(solution)/shard_map/all_gather | solution.py:53
  57.1 4.3 convolution_convert_fusion.1
  61.5 0.1 slice.63
  61.6 0.7 slice_convert_fusion
  62.2 3.5 collective-permute-start
  65.7 0.3 multiply_multiply_fusion.1
  66.0 4.1 collective-permute-done
  70.1 1.0 add_convert_fusion.1
  71.2 3.2 fusion.30
  74.4 1.0 copy.21
  75.4 5.9 %stack.3 = f32[64,1,273,128]{3,1,2,0:T(1,128)} broadcast(f32[273,128]{1,0:T(8,128)S(1)} %copy.21), dimensions={2,3} | broadcast | bytes 9085440 | tf_op jit(solution)/shard_map/stack | solution.py:76
  81.3 15.1 %all-to-all-start = ((f32[64,1,273,128]{3,1,2,0:T(1,128)}), f32[64,1,273,128]{3,1,2,0:T(1,128)}, u32[]{:S(2)}, u32[]{:S(2)}) async-start(f32[64,1,273,128]{3,1,2,0:T(1,128)} %stack.3), calls=%async_computation | async-start | bytes 17891328 | tf_op jit(solution)/shard_map/all_to_all | solution.py:76
  96.4 0.0 reduce-scatter.2.cloned.1.call-start
  96.5 0.1 mul.156
  96.6 0.7 slice.70
  97.3 3.4 collective-permute-start.2
  100.6 0.1 fusion.50
  100.7 0.8 fusion.51
  101.5 1.6 multiply_multiply_fusion
  103.1 1.4 slice.68
  104.5 3.5 collective-permute-start.1
  108.1 0.1 broadcast.172.clone2.1
  108.2 14.3 %while.26 = (s32[]{:T(128)}, f32[2,512,2,64]{1,0,3,2:T(2,128)S(1)}, s32[2]{0:T(128)S(1)}, bf16[1024,2,16]{0,2,1:T(8,128)(2,1)}, bf16[1024,2,16]{0,2,1:T(8,128)(2...) while((s32[]{:T(128)}, f32[2,512,2,64]{1,0,3,2:T(2,128)S(1)}, ...), condition=%wide.region_2.3_spmd.clone, body=%wide.region_1.2_spmd.clone.sunk | while | flops 175636992 | bytes 2724019 | solution.py:102
  108.2 0.6 dynamic_slice.63
  109.5 0.4 iota_compare_fusion.3
  109.9 2.7 fusion.75
  112.6 0.3 copy.37
  112.9 2.4 dynamic_update_slice.17
  115.4 0.6 dynamic_slice.63
  116.7 0.4 iota_compare_fusion.3
  117.0 2.7 fusion.75
  119.8 0.3 copy.37
  120.1 2.4 dynamic_update_slice.17
  122.5 1.2 reshape.151
  123.8 356.9 %collective-permute-done.2 = bf16[63,128]{0,1:T(8,128)(2,1)} collective-permute-done((bf16[63,128]{0,1:T(8,128)(2,1)}, bf16[63,128]{0,1:T(8,128)(2,1)}, u32[]{:S(2)}, u32[]{:S(2)}) %collective-permute-start.2) | collective-permute-done | bytes 16160 | tf_op jit(solution)/shard_map/ppermute | solution.py:15
  480.7 0.9 fusion.48
  481.6 0.9 fusion.49
  482.6 1.1 pad_maximum_fusion
  483.7 0.1 broadcast.172.clone2
  483.8 13.8 %while.27 = (s32[]{:T(128)}, f32[2,512,2,64]{1,0,3,2:T(2,128)S(1)}, s32[2]{0:T(128)S(1)}, bf16[1087,2,64]{0,2,1:T(8,128)(2,1)S(1)}, s32[]{:T(128)}, /*index=5*/b...) while((s32[]{:T(128)}, f32[2,512,2,64]{1,0,3,2:T(2,128)S(1)}, ...), condition=%wide.region_8.9_spmd.clone, body=%wide.region_6.8_spmd.clone.sunk | while | flops 156327104 | bytes 7377774 | solution.py:137
  483.8 0.6 dynamic_slice.67
  485.1 0.2 fusion.77
  485.3 1.9 fusion.78
  487.2 0.8 fusion.79
  488.0 0.3 copy.38
  488.3 2.4 dynamic_update_slice.18
  490.7 0.6 dynamic_slice.67
  492.0 0.2 fusion.77
  492.2 1.9 fusion.78
  494.0 0.8 fusion.79
  494.9 0.3 copy.38
  495.2 2.4 dynamic_update_slice.18
  497.6 0.5 reshape.153
  498.1 0.0 copy-start.1
  498.1 5.4 fusion.29
  503.5 0.1 copy.23
  503.6 0.0 copy-start.2
  503.6 3.7 multiply_reduce_fusion
  507.4 0.1 add_convert_fusion
  507.5 3.2 convolution_convert_fusion
  510.7 0.0 reduce-scatter.2.cloned.1.call-update
  510.8 46.2 %reduce-scatter.2.cloned.1.call-done = bf16[1024,256]{1,0:T(8,128)(2,1)} async-done(((bf16[1024,2048]{1,0:T(8,128)(2,1)}), bf16[1024,256]{1,0:T(8,128)(2,1)}) %reduce-scatter.2.cloned.1.call-update) | async-done | bytes 524304 | tf_op jit(solution)/shard_map/reduce_scatter | solution.py:145
  (22 shorter events, 0.2 us)
Async XLA Ops:
  6.5 50.6 %copy-start = (bf16[2048,448]{0,1:T(8,128)(2,1)S(1)}, bf16[2048,448]{0,1:T(8,128)(2,1)}, u32[]{:S(2)}) copy-start(bf16[2048,448]{0,1:T(8,128)(2,1)} %param.10) | copy-start | bytes 5505028
  6.5 50.6 %all-gather.2.cloned.1.call-start = ((), (), s32[]{:S(2)}) async-start(), calls=%async_computation.2 | async-start | bytes 4718592 | tf_op jit(solution)/shard_map/all_gather | solution.py:53
  62.2 7.9 %collective-permute-start = (bf16[2,128]{0,1:T(8,128)(2,1)S(1)}, bf16[2,128]{0,1:T(8,128)(2,1)S(1)}, u32[]{:S(2)}, u32[]{:S(2)}) collective-permute-start(bf16[2,128]{0,1:T(8,128)(2,1)S(1)} %bitcast.77), channel_id=1, source_target_pairs={{0,8},{8,16},{16,24},{24,32},{32,40},{40,48},{48,56},{56,64},{64,7... | collective-permute-start | bytes 1544 | tf_op jit(solution)/shard_map/ppermute | solution.py:15
  81.3 15.2 %copy-start.3 = (f32[128]{0:T(128)S(1)}, f32[128]{0:T(128)}, u32[]{:S(2)}) copy-start(f32[128]{0:T(128)} %param.12) | copy-start | bytes 1540
  81.3 416.8 %all-to-all-start = ((f32[64,1,273,128]{3,1,2,0:T(1,128)}), f32[64,1,273,128]{3,1,2,0:T(1,128)}, u32[]{:S(2)}, u32[]{:S(2)}) async-start(f32[64,1,273,128]{3,1,2,0:T(1,128)} %stack.3), calls=%async_computation | async-start | bytes 17891328 | tf_op jit(solution)/shard_map/all_to_all | solution.py:76
  96.4 460.5 %reduce-scatter.2.cloned.1.call-start = ((), (), s32[]{:S(2)}) async-start(), calls=%async_computation.3 | async-start | bytes 4718592 | tf_op jit(solution)/shard_map/reduce_scatter | solution.py:145
  97.3 383.4 %collective-permute-start.2 = (bf16[63,128]{0,1:T(8,128)(2,1)}, bf16[63,128]{0,1:T(8,128)(2,1)}, u32[]{:S(2)}, u32[]{:S(2)}) collective-permute-start(bf16[63,128]{0,1:T(8,128)(2,1)} %bitcast.15), channel_id=1, source_target_pairs={{0,8},{8,16},{16,24},{24,32},{32,40},{40,48},{48,56},{56,64},{64,7... | collective-permute-start | bytes 48392 | tf_op jit(solution)/shard_map/ppermute | solution.py:15
  104.5 378.0 %collective-permute-start.1 = (bf16[63,128]{0,1:T(8,128)(2,1)}, bf16[63,128]{0,1:T(8,128)(2,1)}, u32[]{:S(2)}, u32[]{:S(2)}) collective-permute-start(bf16[63,128]{0,1:T(8,128)(2,1)} %slice.68), channel_id=1, source_target_pairs={{0,8},{8,16},{16,24},{24,32},{32,40},{40,48},{48,56},{56,64},{64,7... | collective-permute-start | bytes 48392 | tf_op jit(solution)/shard_map/ppermute | solution.py:15
  498.1 5.5 copy-start.1
  503.6 3.9 copy-start.2
Sparse Core Ops, SparseCore 0:
  9.4 47.6 all-gather.1
  510.9 45.9 reduce-scatter.1
